TPU v7x, 512 devices: a whole 4x4x16 slice. The times are simulated.
512 devices in a mesh: grp: 16 (over z), mod: 32 (over x, y, core).
Axes of the slice: x: 4, y: 4, z: 16, core: 2. Of those that a mesh axis runs over, the one named last changes fastest.
Arguments:
- tokens: bfloat16 [1024, 64, 32, 128], P(('grp', 'mod')), may hold values from -3 to 3
- lengths: int32 [1024], P(('grp', 'mod')), may hold values from 1 to 64, 32768 in all
- module_order: int32 [32], replicated, may hold values from 0 to 31, each once
Outputs:
- preconditioned: float32 [32, 1024, 4096], P('mod', 'grp')
Inputs may be any that keep to these rules, and one draw needn't show every extreme that they name: `lengths`: each example's live tokens are its first slots; some example has exactly 64. `module_order`: each module appears exactly once.
All inputs are finite; a program needn't handle non-finite values. No bound on the sum of `lengths` on one device may be relied on, other than what follows from the above.
Results may differ from a plain program's by a relative error of at most 0.0068.
Values may be sent and summed in bfloat16 or wider, within the bound.
A program may use at most 64 MiB of HBM per device.

v0:
```python
import jax
import jax.numpy as jnp
from jax import lax
from jax.sharding import PartitionSpec as P

ITERS = 3


def partner(value, axis, bit):
    mask = 2**bit
    pairs = [(source, source ^ mask) for source in range(lax.axis_size(axis))]
    return lax.ppermute(value, axis, pairs)


def start_basis(row_count, col_count):
    row_index = jnp.arange(row_count, dtype=jnp.float32)[:, None] + 0.5
    col_index = jnp.arange(col_count, dtype=jnp.float32)[None, :] + 0.5
    return jnp.cos(jnp.pi * row_index * col_index / row_count)


def orthonormal(matrix):
    for repeat in range(2):
        cross_gram = jnp.dot(matrix.T, matrix, precision=lax.Precision.HIGHEST)
        factor = jnp.linalg.cholesky(cross_gram)
        matrix = jax.scipy.linalg.solve_triangular(factor, matrix.T, lower=True).T
    return matrix


def merge_pair(lower_sketch, upper_sketch):
    stacked = jnp.concatenate([lower_sketch, upper_sketch], axis=0)
    kernel = jnp.dot(stacked, stacked.T, precision=lax.Precision.HIGHEST)
    current = start_basis(stacked.shape[0], lower_sketch.shape[0])
    for repeat in range(ITERS):
        current = orthonormal(jnp.dot(kernel, current, precision=lax.Precision.HIGHEST))
    return jnp.dot(current.T, stacked, precision=lax.Precision.HIGHEST)


def precondition(group_rows, sketch):
    sketch_rows = sketch.shape[0]
    damping = 0.1 * jnp.sum(sketch * sketch) / sketch_rows + 1e-06
    capacitance = jnp.dot(sketch, sketch.T, precision=lax.Precision.HIGHEST) + damping * jnp.eye(
        sketch_rows, dtype=jnp.float32
    )
    projected = jnp.dot(group_rows, sketch.T, precision=lax.Precision.HIGHEST)
    factor = jnp.linalg.cholesky(capacitance)
    middle = jax.scipy.linalg.solve_triangular(factor, projected.T, lower=True)
    weights = jax.scipy.linalg.solve_triangular(factor, middle, lower=True, trans=1).T
    return group_rows - jnp.dot(weights, sketch, precision=lax.Precision.HIGHEST)


def local_features(token_block, live_counts):
    example_count, token_slots, module_count, full_width = token_block.shape
    half_width = full_width // 2
    live_mask = jnp.arange(token_slots, dtype=jnp.int32)[None, :] < live_counts[:, None]
    grad_side = jnp.where(
        live_mask[:, :, None, None],
        token_block[:, :, :, half_width:],
        jnp.zeros((), token_block.dtype),
    )
    input_side = token_block[:, :, :, :half_width]
    outer = jnp.einsum("etmo,etmi->meoi", grad_side, input_side, preferred_element_type=jnp.float32)
    return outer.reshape(module_count, example_count, half_width * half_width).astype(jnp.bfloat16)


def per_device(tokens, lengths, module_order):
    picked = jnp.take(tokens, module_order, axis=2)
    regrouped = lax.all_to_all(picked, "mod", split_axis=2, concat_axis=0, tiled=True)
    all_lengths = lax.all_gather(lengths, "mod", axis=0, tiled=True)
    group_rows = local_features(regrouped, all_lengths)
    leaves = group_rows.astype(jnp.float32)
    merge_all = jax.vmap(merge_pair)
    levels = lax.axis_size("grp").bit_length() - 1
    position = lax.axis_index("grp")
    sketch = leaves
    for height in range(levels):
        sister = partner(sketch, "grp", height)
        upper_side = position // 2**height % 2 == 1
        lower_part = jnp.where(upper_side, sister, sketch)
        upper_part = jnp.where(upper_side, sketch, sister)
        sketch = merge_all(lower_part, upper_part)
    return jax.vmap(precondition)(leaves, sketch)


def solution(mesh):
    return jax.shard_map(
        per_device,
        mesh=mesh,
        in_specs=(P(("grp", "mod"), None, None, None), P(("grp", "mod")), P()),
        out_specs=P("mod", "grp", None),
        check_vma=False,
    )
```

profile of v0, /device:TPU:1, one launch (start us, length us, event | category | flops | bytes accessed | tf_op | source)
XLA Modules:
  0.0 652.1 jit_solution(13635535327548843405)
XLA Ops:
  7.6 10.6 %all-to-all-start = ((bf16[2,64,32,128]{3,1,0,2:T(8,128)(2,1)}), bf16[2,64,32,128]{3,1,0,2:T(8,128)(2,1)S(1)}, u32[]{:S(2)}, u32[]{:S(2)}) async-start(bf16[2,64,32,128]{3,1,0,2:T(8,128)(2,1)} %copy.108), calls=%async_computation | async-start | bytes 2097152 | tf_op jit(solution)/shard_map/all_to_all | solution.py:67
  20.5 20.4 %all-reduce = s32[64]{0:T(128)S(1)} all-reduce(s32[64]{0:T(128)S(1)} %dynamic-update-slice.2), channel_id=1, replica_groups=mesh['grp'=16,'mod'=32] {'mod'}, use_global_device_ids=true, to_apply=%add | all-reduce | flops 64 | bytes 512
  45.7 21.1 %collective-permute-done = f32[1,64,4096]{2,1,0:T(8,128)} collective-permute-done((f32[1,64,4096]{2,1,0:T(8,128)S(1)}, f32[1,64,4096]{2,1,0:T(8,128)}, u32[]{:S(2)}, u32[]{:S(2)}) %collective-permute-start) | collective-permute-done | bytes 1048608 | tf_op jit(solution)/shard_map/ppermute | solution.py:12
  83.9 5.8 custom-call.63
  109.6 5.8 custom-call.67
  122.6 5.8 custom-call.69
  135.8 5.8 custom-call.71
  153.4 47.6 %collective-permute-done.1 = f32[1,64,4096]{2,1,0:T(8,128)} collective-permute-done((f32[1,64,4096]{2,1,0:T(8,128)}, f32[1,64,4096]{2,1,0:T(8,128)}, u32[]{:S(2)}, u32[]{:S(2)}) %collective-permute-start.1) | collective-permute-done | bytes 1048608 | tf_op jit(solution)/shard_map/ppermute | solution.py:12
  231.2 5.8 custom-call.77
  243.9 5.8 custom-call.79
  256.9 5.8 custom-call.81
  269.8 5.8 custom-call.83
  284.5 6.5 %collective-permute-start.2 = (f32[1,64,4096]{2,1,0:T(8,128)}, f32[1,64,4096]{2,1,0:T(8,128)}, u32[]{:S(2)}, u32[]{:S(2)}) collective-permute-start(f32[1,64,4096]{2,1,0:T(8,128)} %convolution_bitcast_fusion.1), channel_id=1, source_target_pairs={{0,128},{32,160},{64,192},{96,224},{128,0},{160,32},{192,64},{224,... | collective-permute-start | bytes 3145736 | tf_op jit(solution)/shard_map/ppermute | solution.py:12
  291.1 91.0 %collective-permute-done.2 = f32[1,64,4096]{2,1,0:T(8,128)} collective-permute-done((f32[1,64,4096]{2,1,0:T(8,128)}, f32[1,64,4096]{2,1,0:T(8,128)}, u32[]{:S(2)}, u32[]{:S(2)}) %collective-permute-start.2) | collective-permute-done | bytes 1048608 | tf_op jit(solution)/shard_map/ppermute | solution.py:12
  386.4 5.8 custom-call.85
  399.2 5.8 custom-call.87
  412.2 5.8 custom-call.89
  451.0 5.8 custom-call.95
  465.7 12.3 %collective-permute-start.3 = (f32[1,64,4096]{2,1,0:T(8,128)}, f32[1,64,4096]{2,1,0:T(8,128)S(1)}, u32[]{:S(2)}, u32[]{:S(2)}) collective-permute-start(f32[1,64,4096]{2,1,0:T(8,128)} %convolution_bitcast_fusion), channel_id=1, source_target_pairs={{0,256},{32,288},{64,320},{96,352},{128,384},{160,416},{192,448},{... | collective-permute-start | bytes 3145736 | tf_op jit(solution)/shard_map/ppermute | solution.py:12
  480.7 70.1 %collective-permute-done.3 = f32[1,64,4096]{2,1,0:T(8,128)S(1)} collective-permute-done((f32[1,64,4096]{2,1,0:T(8,128)}, f32[1,64,4096]{2,1,0:T(8,128)S(1)}, u32[]{:S(2)}, u32[]{:S(2)}) %collective-permute-start.3) | collective-permute-done | bytes 1048608 | tf_op jit(solution)/shard_map/ppermute | solution.py:12
  554.8 5.8 custom-call.97
  567.6 5.8 custom-call.99
  580.6 5.8 custom-call.101
  593.3 5.8 custom-call.103
  (266 shorter events, 275.9 us)
Async XLA Ops:
  0.0 1.4 copy-start
  7.6 12.6 %copy-start.5 = (s32[2]{0:T(128)S(1)}, s32[2]{0:T(128)}, u32[]{:S(2)}) copy-start(s32[2]{0:T(128)} %param.7) | copy-start | bytes 28
  7.6 33.4 %all-to-all-start = ((bf16[2,64,32,128]{3,1,0,2:T(8,128)(2,1)}), bf16[2,64,32,128]{3,1,0,2:T(8,128)(2,1)S(1)}, u32[]{:S(2)}, u32[]{:S(2)}) async-start(bf16[2,64,32,128]{3,1,0,2:T(8,128)(2,1)} %copy.108), calls=%async_computation | async-start | bytes 2097152 | tf_op jit(solution)/shard_map/all_to_all | solution.py:67
  42.6 1.0 copy-start.4
  43.5 2.1 copy-start.3
  43.5 23.3 %collective-permute-start = (f32[1,64,4096]{2,1,0:T(8,128)S(1)}, f32[1,64,4096]{2,1,0:T(8,128)}, u32[]{:S(2)}, u32[]{:S(2)}) collective-permute-start(f32[1,64,4096]{2,1,0:T(8,128)S(1)} %reshape.493), channel_id=1, source_target_pairs={{0,32},{32,0},{64,96},{96,64},{128,160},{160,128},{192,224},{224,1... | collective-permute-start | bytes 3145736 | tf_op jit(solution)/shard_map/ppermute | solution.py:12
  150.4 50.6 %collective-permute-start.1 = (f32[1,64,4096]{2,1,0:T(8,128)}, f32[1,64,4096]{2,1,0:T(8,128)}, u32[]{:S(2)}, u32[]{:S(2)}) collective-permute-start(f32[1,64,4096]{2,1,0:T(8,128)} %convolution_bitcast_fusion.2), channel_id=1, source_target_pairs={{0,64},{32,96},{64,0},{96,32},{128,192},{160,224},{192,128},{224,1... | collective-permute-start | bytes 3145736 | tf_op jit(solution)/shard_map/ppermute | solution.py:12
  284.5 97.6 %collective-permute-start.2 = (f32[1,64,4096]{2,1,0:T(8,128)}, f32[1,64,4096]{2,1,0:T(8,128)}, u32[]{:S(2)}, u32[]{:S(2)}) collective-permute-start(f32[1,64,4096]{2,1,0:T(8,128)} %convolution_bitcast_fusion.1), channel_id=1, source_target_pairs={{0,128},{32,160},{64,192},{96,224},{128,0},{160,32},{192,64},{224,... | collective-permute-start | bytes 3145736 | tf_op jit(solution)/shard_map/ppermute | solution.py:12
  465.7 85.1 %collective-permute-start.3 = (f32[1,64,4096]{2,1,0:T(8,128)}, f32[1,64,4096]{2,1,0:T(8,128)S(1)}, u32[]{:S(2)}, u32[]{:S(2)}) collective-permute-start(f32[1,64,4096]{2,1,0:T(8,128)} %convolution_bitcast_fusion), channel_id=1, source_target_pairs={{0,256},{32,288},{64,320},{96,352},{128,384},{160,416},{192,448},{... | collective-permute-start | bytes 3145736 | tf_op jit(solution)/shard_map/ppermute | solution.py:12
  552.2 1.8 copy-start.1
  635.6 13.2 %copy-start.2 = (bf16[64,4096]{1,0:T(8,128)(2,1)S(1)}, bf16[64,4096]{1,0:T(8,128)(2,1)}, u32[]{:S(2)}) copy-start(bf16[64,4096]{1,0:T(8,128)(2,1)} %convert_element_type.37) | copy-start | bytes 1572868
where the time goes:
time: 663 us; the launch traced here: 652 us
  other arithmetic  314 us (47%)
  waiting for transfers between devices  230 us (35%)
  matrix products  37.1 us (6%)
  starting transfers between devices  34.4 us (5%)
  blocking collectives  20.4 us (3%)
  local copies, waits for them, and re-layouts  13.2 us (2%)
    ppermute x4, waiting for transfers between devices, partner(): return lax.ppermute(value, axis, pairs)  230 us
    another operation x72, other arithmetic, orthonormal(): factor = jnp.linalg.cholesky(cross_gram)  158 us
    another operation x48, other arithmetic, orthonormal(): matrix = jax.scipy.linalg.solve_triangular(factor, matrix.T, lower=True).T  135 us
    ppermute x4, starting transfers between devices, partner(): return lax.ppermute(value, axis, pairs)  23.8 us
    unnamed x1, blocking collectives  20.4 us
  transfers between devices with their start and end apart: 5, of which 4 were waited for; matrix products, arithmetic and copies ran while one was open for 1% of the time, Pallas kernels for 0%

commit v1 on v0

v1 whole, which is shorter than its diff:
```python
import functools

import jax
import jax.numpy as jnp
import numpy as np
from jax import lax
from jax.experimental import pallas as pl
from jax.experimental.pallas import tpu as pltpu
from jax.sharding import PartitionSpec as P

ITERS = 3
F32 = jnp.float32
BF16 = jnp.bfloat16
EXACT = lax.Precision.HIGHEST
VMEM = pltpu.MemorySpace.VMEM
SMEM = pltpu.MemorySpace.SMEM


def start_rows(row_count, col_count):
    row_index = np.arange(row_count, dtype=np.float64)[None, :] + 0.5
    col_index = np.arange(col_count, dtype=np.float64)[:, None] + 0.5
    return np.cos(np.pi * row_index * col_index / row_count).astype(np.float32)


def mm(a, b):
    return lax.dot_general(a, b, (((1,), (0,)), ((), ())), precision=EXACT, preferred_element_type=F32)


def mm_nt(a, b):
    return lax.dot_general(a, b, (((1,), (1,)), ((), ())), precision=EXACT, preferred_element_type=F32)


def bmm(a, b):
    return lax.dot_general(a, b, (((1,), (0,)), ((), ())), preferred_element_type=F32)


def bmm_nt(a, b):
    return lax.dot_general(a, b, (((1,), (1,)), ((), ())), preferred_element_type=F32)


def split2(x):
    hi = x.astype(BF16)
    return hi, (x - hi.astype(F32)).astype(BF16)


def split3(x):
    hi, rest = x.astype(BF16), None
    rest = x - hi.astype(F32)
    mid = rest.astype(BF16)
    return hi, mid, (rest - mid.astype(F32)).astype(BF16)


def eliminate(gram, rows):
    size = gram.shape[0]
    blocks = size // 8
    sub = lax.broadcasted_iota(jnp.int32, (8, 128), 0)
    padded = jnp.concatenate([gram, jnp.zeros((size, 128 - size), F32)], axis=1)
    left = [padded[8 * i : 8 * i + 8] for i in range(blocks)]
    right = [rows[8 * i : 8 * i + 8] for i in range(blocks)]

    def along_lanes(x, lane):
        return jnp.broadcast_to(x[:, lane : lane + 1], (8, 128))

    def along_rows(x, row):
        return jnp.broadcast_to(x[row : row + 1, :], (8, 128))

    done = []
    for k in range(blocks):
        p_left, p_right = left[k], right[k]
        cols = [along_lanes(p_left, 8 * k + c) for c in range(8)]
        below = {i: [along_lanes(left[i], 8 * k + c) for c in range(8)] for i in range(k + 1, blocks)}
        pivots = jnp.ones((8, 128), F32)
        reduced = jnp.zeros((8, 128), F32)
        for j in range(8):
            col = cols[j]
            pivot = along_rows(col, j)
            inverse = 1.0 / pivot
            here = sub == j
            pivots = jnp.where(here, pivot, pivots)
            row_right = along_rows(p_right, j)
            reduced = jnp.where(here, row_right, reduced)
            for c in range(j + 1, 8):
                scaled = along_rows(cols[c], j) * inverse
                cols[c] = jnp.where(here, scaled, cols[c] - col * scaled)
            scaled = along_rows(p_left, j) * inverse
            p_left = jnp.where(here, scaled, p_left - col * scaled)
            scaled = row_right * inverse
            p_right = jnp.where(here, scaled, p_right - col * scaled)
        done.append(reduced * lax.rsqrt(pivots))
        for c in range(8):
            row_left, row_right = along_rows(p_left, c), along_rows(p_right, c)
            for i in range(k + 1, blocks):
                left[i] = left[i] - below[i][c] * row_left
                right[i] = right[i] - below[i][c] * row_right
    return jnp.concatenate(done, axis=0)


def basis_of(kernel, start):
    def step(_, basis):
        image = mm(basis, kernel)
        return eliminate(mm_nt(image, image), image)

    basis = lax.fori_loop(0, ITERS, step, start)
    gram = mm_nt(basis, basis)
    row = lax.broadcasted_iota(jnp.int32, gram.shape, 0)
    col = lax.broadcasted_iota(jnp.int32, gram.shape, 1)
    fix = jnp.where(row > col, gram, 0.0) + jnp.where(row == col, 0.5 * (gram - 1.0), 0.0)
    basis = basis - mm(fix, basis)
    return basis, mm_nt(mm(basis, kernel), basis)


def pack(x):
    return jnp.concatenate([x[:32], x[32:]], axis=1)


def unpack(x):
    return jnp.concatenate([x[:, :64], x[:, 64:]], axis=0)


def assemble(lower, cross, upper):
    top = jnp.concatenate([lower, cross], axis=1)
    return jnp.concatenate([top, jnp.concatenate([cross.T, upper], axis=1)], axis=0)


def split_basis(basis):
    hi, lo = split2(basis)
    zero = jnp.zeros((64, 64), BF16)
    top = jnp.concatenate([hi[:, :64], hi[:, :64], hi[:, 64:], hi[:, 64:]], axis=1)
    low = jnp.concatenate([lo[:, :64], zero, lo[:, 64:], zero], axis=1)
    return jnp.concatenate([top, low], axis=0)


def feature_kernel(lengths, order, tokens, out):
    def one(slot, carry):
        module = order[slot]
        for example in range(2):
            x = tokens[module, example]
            live = lax.broadcasted_iota(jnp.int32, x.shape, 0) < lengths[example]
            x = jnp.where(live, x.astype(F32), 0.0).astype(BF16)
            outer = lax.dot_general(x, x, (((0,), (0,)), ((), ())), preferred_element_type=F32)
            both = jnp.concatenate([outer[64:96, :64], outer[96:, :64]], axis=1)
            out[slot, example] = both.astype(BF16)
        return carry

    lax.fori_loop(0, 32, one, 0)


def tree_kernel(
    leaf, start, out,
    pair, quad, slab1, slab2, slab3, send2,
    d0_out, d0_in, qd_out, qd_in, d2_out, d2_in,
    x0, x1, x2,
    bulk_send, bulk_recv, small_send, small_recv,
    x0_send, x0_recv, x1_send, x1_recv, x2_send, x2_recv,
    right_send, right_recv, left_send, left_recv,
):
    me = lax.axis_index("grp")
    b0, b1, b2 = me % 2, (me // 2) % 2, (me // 4) % 2
    sister0 = me + 1 - 2 * b0
    sister1 = me + 2 - 4 * b1
    sister2 = me + 4 - 8 * b2

    def to(index):
        return dict(device_id={"grp": index}, device_id_type=pl.DeviceIdType.MESH)

    def send(src, dst, sems, recvs, slot_send, slot_recv, index):
        copy = pltpu.make_async_remote_copy(
            src_ref=src, dst_ref=dst, send_sem=sems.at[slot_send], recv_sem=recvs.at[slot_recv], **to(index)
        )
        copy.start()
        return copy

    barrier = pltpu.get_barrier_semaphore()
    for d in range(1, 16):
        pl.semaphore_signal(barrier, inc=1, **to((me + d) % 16))
    pl.semaphore_wait(barrier, 15)

    leaf_copy = send(
        leaf.at[pl.ds((1 - b0) * 16, 16)], pair.at[:, pl.ds(b0 * 64, 64), :],
        bulk_send, bulk_recv, 0, 0, sister0,
    )

    def own_gram(r, acc):
        slab = leaf[r]
        return acc + bmm_nt(slab, slab)

    d_own = lax.fori_loop(0, 32, own_gram, jnp.zeros((64, 64), F32), unroll=8)
    d0_out[...] = pack(d_own)
    d_copy = send(d0_out, d0_in, small_send, small_recv, 0, 0, sister0)
    pair[:, pl.ds(b0 * 64, 64), :] = leaf[pl.ds(b0 * 16, 16)]

    early = []
    for other in range(2):
        target = sister1 - b0 + other
        offset = other * 16 + (1 - b1) * 8
        early.append((
            leaf.at[pl.ds(offset, 8)], quad.at[:, pl.ds(b0 * 64, 64), :],
            bulk_send, bulk_recv, 1 + other, 1 + b0, target,
        ))
    leaf_copy.wait()
    early = [send(*args) for args in early]
    d_copy.wait()

    def reduce_cross(partial, box, sems, recvs, members):
        mine = me % members
        base = me - mine
        box[mine] = pack(partial)
        copies = [
            send(box.at[mine], box.at[mine], sems, recvs, d, mine, base + (mine + d) % members)
            for d in range(1, members)
        ]
        for copy in copies:
            copy.wait_send()
        for d in range(1, members):
            source = (mine + d) % members
            pltpu.make_async_remote_copy(
                src_ref=box.at[source], dst_ref=box.at[source], send_sem=sems.at[d],
                recv_sem=recvs.at[source], **to(base + source)
            ).wait_recv()
        total = box[0]
        for i in range(1, members):
            total = total + box[i]
        return unpack(total)

    def cross0(r, acc):
        slab = pair[r]
        return acc + bmm_nt(slab[:64], slab[64:])

    cross = lax.fori_loop(0, 16, cross0, jnp.zeros((64, 64), F32), unroll=8)
    cross = reduce_cross(cross, x0, x0_send, x0_recv, 2)
    d_sister = unpack(d0_in[...])
    kernel = assemble(jnp.where(b0 == 0, d_own, d_sister), cross, jnp.where(b0 == 0, d_sister, d_own))
    basis, d_own = basis_of(kernel, start[...])
    qd_out[:64] = basis
    qd_out[64:] = pack(d_own)
    qd_copy = send(qd_out, qd_in, small_send, small_recv, 1, 1, sister1)

    def merged0(b, slabs, first, side):
        operand = jnp.concatenate(split3(b), axis=0)

        def one(r, carry):
            product = bmm(operand, slabs[first + r])
            product = product[:64] + product[64:128] + product[128:]
            hi, lo = split2(product)
            slab1[r, pl.ds(side * 128, 64), :] = hi
            slab1[r, pl.ds(side * 128 + 64, 64), :] = lo
            return carry

        lax.fori_loop(0, 8, one, 0, unroll=4)

    merged0(basis, pair, b1 * 8, b1)
    for copy in early:
        copy.wait_send()
    for other in range(2):
        pltpu.make_async_remote_copy(
            src_ref=leaf.at[pl.ds(0, 8)], dst_ref=quad.at[:, pl.ds(other * 64, 64), :],
            send_sem=bulk_send.at[1 + other], recv_sem=bulk_recv.at[1 + other], **to(sister1 - b0 + other)
        ).wait_recv()
    qd_copy.wait()
    merged0(qd_in[:64], quad, 0, 1 - b1)
    d_sister = unpack(qd_in[64:])

    def cross_of(slabs, count):
        def one(r, acc):
            slab = slabs[r]
            return acc + bmm_nt(slab[:128], slab[128:])

        acc = lax.fori_loop(0, count, one, jnp.zeros((128, 128), F32), unroll=4)
        return acc[:64, :64] + acc[:64, 64:] + acc[64:, :64] + acc[64:, 64:]

    cross = reduce_cross(cross_of(slab1, 8), x1, x1_send, x1_recv, 4)
    kernel = assemble(jnp.where(b1 == 0, d_own, d_sister), cross, jnp.where(b1 == 0, d_sister, d_own))
    basis, d_own = basis_of(kernel, start[...])
    d2_out[...] = pack(d_own)
    d_copy = send(d2_out, d2_in, small_send, small_recv, 2, 2, sister2)

    def merged(operand, slab):
        product = bmm(operand, slab)
        return product[:64] + product[64:]

    operand = split_basis(basis)
    for r in range(4):
        hi, lo = split2(merged(operand, slab1[(1 - b2) * 4 + r]))
        send2[r, :64] = hi
        send2[r, 64:] = lo
    slab_copy = send(send2, slab2.at[:, pl.ds(b2 * 128, 128), :], bulk_send, bulk_recv, 3, 3, sister2)
    for r in range(4):
        hi, lo = split2(merged(operand, slab1[b2 * 4 + r]))
        slab2[r, pl.ds(b2 * 128, 64), :] = hi
        slab2[r, pl.ds(b2 * 128 + 64, 64), :] = lo
    slab_copy.wait()
    d_copy.wait()
    d_sister = unpack(d2_in[...])
    cross = reduce_cross(cross_of(slab2, 4), x2, x2_send, x2_recv, 8)
    kernel = assemble(jnp.where(b2 == 0, d_own, d_sister), cross, jnp.where(b2 == 0, d_sister, d_own))
    basis, _ = basis_of(kernel, start[...])

    operand = split_basis(basis)
    column, side = me % 8, me // 8
    for r in range(4):
        hi, lo = split2(merged(operand, slab2[r]))
        slab3[column, r, pl.ds(side * 128, 64), :] = hi
        slab3[column, r, pl.ds(side * 128 + 64, 64), :] = lo

    right, left = (me + 1) % 16, (me + 15) % 16

    def part(index, half):
        index = index % 16
        return slab3.at[index % 8, pl.ds(half * 2, 2), pl.ds(index // 8 * 128, 128), :]

    def hop(step, half, rightward):
        origin = me + 16 - (step - 1) if rightward else me + (step - 1)
        sems, recvs = (right_send, right_recv) if rightward else (left_send, left_recv)
        slot = (step - 1) * 2 + half
        ref = part(origin, half)
        return pltpu.make_async_remote_copy(
            src_ref=ref, dst_ref=ref, send_sem=sems.at[slot], recv_sem=recvs.at[slot],
            **to(right if rightward else left)
        )

    def landed(step, half, rightward):
        origin = me + 16 - step if rightward else me + step
        sems, recvs = (right_send, right_recv) if rightward else (left_send, left_recv)
        slot = (step - 1) * 2 + half
        ref = part(origin, half)
        return pltpu.make_async_remote_copy(
            src_ref=ref, dst_ref=ref, send_sem=sems.at[slot], recv_sem=recvs.at[slot],
            **to(right if rightward else left)
        )

    def travels(step, half, rightward):
        return step < 8 or (half == 0) == rightward

    for step in range(1, 9):
        for half in range(2):
            for rightward in (True, False):
                if step > 1 and travels(step - 1, half, rightward):
                    landed(step - 1, half, rightward).wait_recv()
                if travels(step, half, rightward):
                    hop(step, half, rightward).start()
    landed(8, 0, True).wait_recv()
    landed(8, 1, False).wait_recv()
    for step in range(1, 9):
        for half in range(2):
            for rightward in (True, False):
                if travels(step, half, rightward):
                    hop(step, half, rightward).wait_send()

    def first_row(c):
        return (c % 2) * 16 + (c // 2 % 2) * 8 + (c // 4) * 4

    def grams(c, carry):
        gram, along = carry
        for r in range(4):
            slab = slab3[c, r]
            gram = gram + bmm_nt(slab, slab)
            along = along + bmm_nt(leaf[first_row(c) + r], slab)
        return gram, along

    gram, along = lax.fori_loop(
        0, 8, grams, (jnp.zeros((256, 256), F32), jnp.zeros((64, 256), F32))
    )
    gram = jnp.concatenate([gram[:64] + gram[64:128], gram[128:192] + gram[192:]], axis=0)
    kernel = jnp.concatenate(
        [gram[:, :64] + gram[:, 64:128], gram[:, 128:192] + gram[:, 192:]], axis=1
    )
    along = jnp.concatenate(
        [along[:, :64] + along[:, 64:128], along[:, 128:192] + along[:, 192:]], axis=1
    )
    basis, d_final = basis_of(kernel, start[...])

    row = lax.broadcasted_iota(jnp.int32, (64, 64), 0)
    col = lax.broadcasted_iota(jnp.int32, (64, 64), 1)
    eye = jnp.where(row == col, 1.0, 0.0)
    damping = 0.1 * jnp.sum(d_final * eye, keepdims=True) / 64 + 1e-06
    capacitance = d_final + damping * eye
    inverse = eliminate(capacitance, jnp.concatenate([eye, jnp.zeros((64, 64), F32)], axis=1))[:, :64]
    projected = mm_nt(along, basis)
    weights = mm(mm_nt(projected, inverse), inverse)
    operand = split_basis(mm(weights, basis))

    def finish(c, carry):
        first = first_row(c)
        for r in range(0, 4, 2):
            one = leaf[first + r].astype(F32) - merged(operand, slab3[c, r])
            two = leaf[first + r + 1].astype(F32) - merged(operand, slab3[c, r + 1])
            where = (first + r) // 2
            out[:, pl.ds(pl.multiple_of(where * 128, 128), 128)] = jnp.concatenate([one[:, :64], two[:, :64]], axis=1)
            out[:, pl.ds(pl.multiple_of((where + 16) * 128, 128), 128)] = jnp.concatenate([one[:, 64:], two[:, 64:]], axis=1)
        return carry

    lax.fori_loop(0, 8, finish, 0)


def per_device(tokens, lengths, module_order):
    by_module = jnp.transpose(tokens, (2, 0, 1, 3))
    features = pl.pallas_call(
        feature_kernel,
        out_shape=jax.ShapeDtypeStruct((32, 2, 32, 128), BF16),
        in_specs=[pl.BlockSpec(memory_space=SMEM)] * 2 + [pl.BlockSpec(memory_space=VMEM)],
        out_specs=pl.BlockSpec(memory_space=VMEM),
        name="features",
    )(lengths, module_order, by_module)
    rows = lax.all_to_all(features, "mod", split_axis=0, concat_axis=0, tiled=True)
    leaf = jnp.transpose(rows.reshape(64, 32, 128), (1, 0, 2))
    dma = pltpu.SemaphoreType.DMA
    result = pl.pallas_call(
        tree_kernel,
        out_shape=jax.ShapeDtypeStruct((64, 4096), F32),
        in_specs=[pl.BlockSpec(memory_space=VMEM)] * 2,
        out_specs=pl.BlockSpec(memory_space=VMEM),
        scratch_shapes=[
            pltpu.VMEM((16, 128, 128), BF16),
            pltpu.VMEM((8, 128, 128), BF16),
            pltpu.VMEM((8, 256, 128), BF16),
            pltpu.VMEM((4, 256, 128), BF16),
            pltpu.VMEM((8, 4, 256, 128), BF16),
            pltpu.VMEM((4, 128, 128), BF16),
            pltpu.VMEM((32, 128), F32),
            pltpu.VMEM((32, 128), F32),
            pltpu.VMEM((96, 128), F32),
            pltpu.VMEM((96, 128), F32),
            pltpu.VMEM((32, 128), F32),
            pltpu.VMEM((32, 128), F32),
            pltpu.VMEM((2, 32, 128), F32),
            pltpu.VMEM((4, 32, 128), F32),
            pltpu.VMEM((8, 32, 128), F32),
            dma((4,)), dma((4,)), dma((3,)), dma((3,)),
            dma((2,)), dma((2,)), dma((4,)), dma((4,)), dma((8,)), dma((8,)),
            dma((16,)), dma((16,)), dma((16,)), dma((16,)),
        ],
        compiler_params=pltpu.CompilerParams(collective_id=0, has_side_effects=True),
        name="tree",
    )(leaf, jnp.asarray(start_rows(128, 64)))
    return result[None]


def solution(mesh):
    return jax.shard_map(
        per_device,
        mesh=mesh,
        in_specs=(P(("grp", "mod"), None, None, None), P(("grp", "mod")), P()),
        out_specs=P("mod", "grp", None),
        check_vma=False,
    )
```

time: 663 us -> 172 us (0.26)
  the two profiles are of different devices: /device:TPU:1 before, /device:TPU:32 now
where the time goes in v1:
time: 172 us
  Pallas kernels  147 us (85%)
  blocking collectives  18.4 us (11%)
  local copies, waits for them, and re-layouts  6.21 us (4%)
    pallas_call x1, Pallas kernels, per_device(): pl.pallas_call(tree_kernel, out_shape=jax.ShapeDtypeStruct((64, 4096), F3...  136 us
    all_to_all x1, blocking collectives, per_device(): lax.all_to_all(features, 'mod', split_axis=0, concat_axis=0, tiled=True)  18.4 us
    pallas_call x1, Pallas kernels, per_device(): pl.pallas_call(feature_kernel, out_shape=jax.ShapeDtypeStruct((32, 2, 32,...  10.9 us
    unnamed x2, local copies, waits for them, and re-layouts  4.87 us

profile of v1, /device:TPU:32, one launch (start us, length us, event | category | flops | bytes accessed | tf_op | source)
XLA Modules:
  0.0 171.6 jit_solution(4559496233928352616)
XLA Ops:
  0.0 2.6 %copy.8 = bf16[2,64,32,128]{3,1,0,2:T(8,128)(2,1)} copy(bf16[2,64,32,128]{3,2,1,0:T(8,128)(2,1)} %param.4) | data formatting | bytes 2097152 | tf_op args[0]
  2.6 10.9 %features.1 = bf16[32,2,32,128]{3,2,1,0:T(8,128)(2,1)} custom-call(s32[2]{0:T(128)} %lengths.1, s32[32]{0:T(128)} %order.1, bf16[32,2,64,128]{3,2,1,0:T(8,128)(2,1)} %bitcast.8), custom_call_target="tpu_custom_call" | custom-call | tf_op jit(solution)/shard_map/features/pallas_call | solution.py:397
  13.5 18.4 %all_to_all.5 = bf16[32,2,32,128]{3,2,1,0:T(8,128)(2,1)S(1)} all-to-all(bf16[32,2,32,128]{3,2,1,0:T(8,128)(2,1)} %features.1), channel_id=1, replica_groups=mesh['grp'=16,'mod'=32] {'mod'}, dimensions={0} | all-to-all | bytes 1048576 | tf_op jit(solution)/shard_map/all_to_all | solution.py:404
  31.9 1.3 copy.6
  33.3 136.1 %tree.1 = f32[64,4096]{1,0:T(8,128)} custom-call(bf16[32,64,128]{2,1,0:T(8,128)(2,1)} %bitcast.9, f32[64,128]{1,0:T(8,128)} %constant.2.clone.start), custom_call_target="tpu_custom_call" | custom-call | tf_op jit(solution)/shard_map/tree/pallas_call | solution.py:407
  169.3 2.3 %copy.10 = f32[1,64,4096]{2,1,0:T(8,128)} copy(f32[1,64,4096]{2,1,0:T(8,128)} %bitcast.7) | data formatting | bytes 2097152

commit v2 on v1

--- a/solution.py
+++ b/solution.py
@@ -101,11 +101,6 @@
         return eliminate(mm_nt(image, image), image)
 
     basis = lax.fori_loop(0, ITERS, step, start)
-    gram = mm_nt(basis, basis)
-    row = lax.broadcasted_iota(jnp.int32, gram.shape, 0)
-    col = lax.broadcasted_iota(jnp.int32, gram.shape, 1)
-    fix = jnp.where(row > col, gram, 0.0) + jnp.where(row == col, 0.5 * (gram - 1.0), 0.0)
-    basis = basis - mm(fix, basis)
     return basis, mm_nt(mm(basis, kernel), basis)
 
 
@@ -130,31 +125,67 @@
     return jnp.concatenate([top, low], axis=0)
 
 
-def feature_kernel(lengths, order, tokens, out):
-    def one(slot, carry):
-        module = order[slot]
-        for example in range(2):
-            x = tokens[module, example]
-            live = lax.broadcasted_iota(jnp.int32, x.shape, 0) < lengths[example]
-            x = jnp.where(live, x.astype(F32), 0.0).astype(BF16)
-            outer = lax.dot_general(x, x, (((0,), (0,)), ((), ())), preferred_element_type=F32)
-            both = jnp.concatenate([outer[64:96, :64], outer[96:, :64]], axis=1)
-            out[slot, example] = both.astype(BF16)
-        return carry
-
-    lax.fori_loop(0, 32, one, 0)
+def features_of(x, live):
+    zero = jnp.zeros((), x.dtype)
+    x = jnp.where(live, x, zero)
+    gradient = x.T[64:]
+    lane = lax.broadcasted_iota(jnp.int32, gradient.shape, 1)
+    sides = jnp.concatenate([jnp.where(lane < 64, gradient, zero), jnp.where(lane >= 64, gradient, zero)], axis=0)
+    outer = bmm(sides, x)
+    return [
+        jnp.concatenate([outer[first : first + 32, :64], outer[first + 32 : first + 64, :64]], axis=1).astype(BF16)
+        for first in (0, 64)
+    ]
+
+
+class Ring:
+    def __init__(self, me, slabs, sems, to):
+        self.me, self.slabs, self.to = me, slabs, to
+        self.sems = {True: sems[:2], False: sems[2:]}
+
+    def copy(self, step, part, rightward, arriving):
+        behind = step if arriving else step - 1
+        origin = (self.me + 16 - behind if rightward else self.me + behind) % 16
+        ref = self.slabs.at[origin % 8, part, pl.ds(origin // 8 * 128, 128), :]
+        send, recv = self.sems[rightward]
+        slot = (step - 1) * 4 + part
+        return pltpu.make_async_remote_copy(
+            src_ref=ref, dst_ref=ref, send_sem=send.at[slot], recv_sem=recv.at[slot],
+            **self.to((self.me + (1 if rightward else 15)) % 16)
+        )
+
+    @staticmethod
+    def travels(step, part, rightward):
+        return step < 8 or (part < 2) == rightward
+
+    def advance(self, step):
+        for part in range(4):
+            for rightward in (True, False):
+                if step > 1 and self.travels(step - 1, part, rightward):
+                    self.copy(step - 1, part, rightward, True).wait_recv()
+                if step < 9 and self.travels(step, part, rightward):
+                    self.copy(step, part, rightward, False).start()
+
+    def drain(self):
+        for step in range(1, 9):
+            for part in range(4):
+                for rightward in (True, False):
+                    if self.travels(step, part, rightward):
+                        self.copy(step, part, rightward, False).wait_send()
 
 
 def tree_kernel(
-    leaf, start, out,
-    pair, quad, slab1, slab2, slab3, send2,
+    lengths, order, tokens, start, out,
+    by_module, features, rows, leaf,
+    pair, quad, slab1, slab2, slab3, send2h, send2l, along,
     d0_out, d0_in, qd_out, qd_in, d2_out, d2_in,
-    x0, x1, x2,
+    x0, x1, x2, wide,
+    to_owner, at_owner,
     bulk_send, bulk_recv, small_send, small_recv,
     x0_send, x0_recv, x1_send, x1_recv, x2_send, x2_recv,
-    right_send, right_recv, left_send, left_recv,
+    *ring_sems,
 ):
-    me = lax.axis_index("grp")
+    me, owner = lax.axis_index("grp"), lax.axis_index("mod")
     b0, b1, b2 = me % 2, (me // 2) % 2, (me // 4) % 2
     sister0 = me + 1 - 2 * b0
     sister1 = me + 2 - 4 * b1
@@ -162,6 +193,9 @@
 
     def to(index):
         return dict(device_id={"grp": index}, device_id_type=pl.DeviceIdType.MESH)
+
+    def across(index):
+        return dict(device_id={"mod": index}, device_id_type=pl.DeviceIdType.MESH)
 
     def send(src, dst, sems, recvs, slot_send, slot_recv, index):
         copy = pltpu.make_async_remote_copy(
@@ -171,14 +205,79 @@
         return copy
 
     barrier = pltpu.get_barrier_semaphore()
-    for d in range(1, 16):
-        pl.semaphore_signal(barrier, inc=1, **to((me + d) % 16))
-    pl.semaphore_wait(barrier, 15)
+
+    def greet(d, carry):
+        pl.semaphore_signal(barrier, inc=1, **across((owner + d) % 32))
+        return carry
+
+    lax.fori_loop(1, 32, greet, 0)
+    for d in range(1, 8):
+        pl.semaphore_signal(barrier, inc=1, **to(me // 8 * 8 + (me + d) % 8))
+    pl.semaphore_signal(barrier, inc=1, **to((me + 1) % 16))
+    pl.semaphore_signal(barrier, inc=1, **to((me + 15) % 16))
+
+    for example in range(2):
+        by_module[:, pl.ds(example * 64, 64), :] = jnp.transpose(tokens[example], (1, 0, 2))
+    token = lax.broadcasted_iota(jnp.int32, (128, 128), 0)
+    live = token < jnp.where(token < 64, lengths[0], 64 + lengths[1])
+
+    def make(group, carry):
+        for i in range(16):
+            slot = group * 16 + i
+            first, second = features_of(by_module[order[slot]], live)
+            features[slot, 0] = first
+            features[slot, 1] = second
+        return carry
+
+    lax.fori_loop(0, 2, make, 0)
+    pl.semaphore_wait(barrier, 40)
+
+    def delivery(d, half):
+        target = (owner + d) % 32
+        columns = pl.ds(half * 16, 16)
+        return pltpu.make_async_remote_copy(
+            src_ref=features.at[target, :, columns], dst_ref=rows.at[pl.ds(owner * 2, 2), columns],
+            send_sem=to_owner.at[half, target], recv_sem=at_owner.at[half, owner], **across(target)
+        )
+
+    def arrival(d, half):
+        source = (owner + d) % 32
+        columns = pl.ds(half * 16, 16)
+        return pltpu.make_async_remote_copy(
+            src_ref=features.at[source, :, columns], dst_ref=rows.at[pl.ds(source * 2, 2), columns],
+            send_sem=to_owner.at[half, source], recv_sem=at_owner.at[half, source], **across(source)
+        )
+
+    for half in (1 - b0, b0):
+        def deliver(d, carry):
+            delivery(d, half).start()
+            return carry
+
+        lax.fori_loop(1, 32, deliver, 0)
+    rows[pl.ds(owner * 2, 2)] = features[owner]
+
+    def collect(half):
+        def one(d, carry):
+            arrival(d, half).wait_recv()
+            return carry
+
+        lax.fori_loop(1, 32, one, 0)
+        leaf[pl.ds(half * 16, 16)] = jnp.transpose(rows[:, pl.ds(half * 16, 16)], (1, 0, 2))
+
+    collect(1 - b0)
 
     leaf_copy = send(
         leaf.at[pl.ds((1 - b0) * 16, 16)], pair.at[:, pl.ds(b0 * 64, 64), :],
         bulk_send, bulk_recv, 0, 0, sister0,
     )
+    collect(b0)
+
+    def sent(d, carry):
+        delivery(d, 0).wait_send()
+        delivery(d, 1).wait_send()
+        return carry
+
+    lax.fori_loop(1, 32, sent, 0)
 
     def own_gram(r, acc):
         slab = leaf[r]
@@ -260,19 +359,16 @@
     merged0(qd_in[:64], quad, 0, 1 - b1)
     d_sister = unpack(qd_in[64:])
 
-    def cross_of(slabs, count):
-        def one(r, acc):
-            slab = slabs[r]
-            return acc + bmm_nt(slab[:128], slab[128:])
-
-        acc = lax.fori_loop(0, count, one, jnp.zeros((128, 128), F32), unroll=4)
-        return acc[:64, :64] + acc[:64, 64:] + acc[64:, :64] + acc[64:, 64:]
-
-    cross = reduce_cross(cross_of(slab1, 8), x1, x1_send, x1_recv, 4)
+    def cross1(r, acc):
+        slab = slab1[r]
+        return acc + bmm_nt(slab[:128], slab[128:])
+
+    acc = lax.fori_loop(0, 8, cross1, jnp.zeros((128, 128), F32), unroll=4)
+    cross = acc[:64, :64] + acc[:64, 64:] + acc[64:, :64] + acc[64:, 64:]
+    cross = reduce_cross(cross, x1, x1_send, x1_recv, 4)
     kernel = assemble(jnp.where(b1 == 0, d_own, d_sister), cross, jnp.where(b1 == 0, d_sister, d_own))
     basis, d_own = basis_of(kernel, start[...])
     d2_out[...] = pack(d_own)
-    d_copy = send(d2_out, d2_in, small_send, small_recv, 2, 2, sister2)
 
     def merged(operand, slab):
         product = bmm(operand, slab)
@@ -281,19 +377,25 @@
     operand = split_basis(basis)
     for r in range(4):
         hi, lo = split2(merged(operand, slab1[(1 - b2) * 4 + r]))
-        send2[r, :64] = hi
-        send2[r, 64:] = lo
-    slab_copy = send(send2, slab2.at[:, pl.ds(b2 * 128, 128), :], bulk_send, bulk_recv, 3, 3, sister2)
+        send2h[r] = hi
+        send2l[r] = lo
+    hi_copy = send(send2h, slab2.at[:, pl.ds(b2 * 128, 64), :], bulk_send, bulk_recv, 3, 3, sister2)
+    d_copy = send(d2_out, d2_in, small_send, small_recv, 2, 2, sister2)
     for r in range(4):
         hi, lo = split2(merged(operand, slab1[b2 * 4 + r]))
         slab2[r, pl.ds(b2 * 128, 64), :] = hi
         slab2[r, pl.ds(b2 * 128 + 64, 64), :] = lo
-    slab_copy.wait()
+    hi_copy.wait()
     d_copy.wait()
     d_sister = unpack(d2_in[...])
-    cross = reduce_cross(cross_of(slab2, 4), x2, x2_send, x2_recv, 8)
+    cross = jnp.zeros((64, 64), F32)
+    for r in range(4):
+        cross = cross + bmm_nt(slab2[r, :64], slab2[r, 128:192])
+    cross = reduce_cross(cross, x2, x2_send, x2_recv, 8)
+    lo_copy = send(send2l, slab2.at[:, pl.ds(b2 * 128 + 64, 64), :], bulk_send, bulk_recv, 4, 4, sister2)
     kernel = assemble(jnp.where(b2 == 0, d_own, d_sister), cross, jnp.where(b2 == 0, d_sister, d_own))
     basis, _ = basis_of(kernel, start[...])
+    lo_copy.wait()
 
     operand = split_basis(basis)
     column, side = me % 8, me // 8
@@ -302,70 +404,43 @@
         slab3[column, r, pl.ds(side * 128, 64), :] = hi
         slab3[column, r, pl.ds(side * 128 + 64, 64), :] = lo
 
-    right, left = (me + 1) % 16, (me + 15) % 16
-
-    def part(index, half):
-        index = index % 16
-        return slab3.at[index % 8, pl.ds(half * 2, 2), pl.ds(index // 8 * 128, 128), :]
-
-    def hop(step, half, rightward):
-        origin = me + 16 - (step - 1) if rightward else me + (step - 1)
-        sems, recvs = (right_send, right_recv) if rightward else (left_send, left_recv)
-        slot = (step - 1) * 2 + half
-        ref = part(origin, half)
-        return pltpu.make_async_remote_copy(
-            src_ref=ref, dst_ref=ref, send_sem=sems.at[slot], recv_sem=recvs.at[slot],
-            **to(right if rightward else left)
-        )
-
-    def landed(step, half, rightward):
-        origin = me + 16 - step if rightward else me + step
-        sems, recvs = (right_send, right_recv) if rightward else (left_send, left_recv)
-        slot = (step - 1) * 2 + half
-        ref = part(origin, half)
-        return pltpu.make_async_remote_copy(
-            src_ref=ref, dst_ref=ref, send_sem=sems.at[slot], recv_sem=recvs.at[slot],
-            **to(right if rightward else left)
-        )
-
-    def travels(step, half, rightward):
-        return step < 8 or (half == 0) == rightward
-
-    for step in range(1, 9):
-        for half in range(2):
-            for rightward in (True, False):
-                if step > 1 and travels(step - 1, half, rightward):
-                    landed(step - 1, half, rightward).wait_recv()
-                if travels(step, half, rightward):
-                    hop(step, half, rightward).start()
-    landed(8, 0, True).wait_recv()
-    landed(8, 1, False).wait_recv()
-    for step in range(1, 9):
-        for half in range(2):
-            for rightward in (True, False):
-                if travels(step, half, rightward):
-                    hop(step, half, rightward).wait_send()
-
     def first_row(c):
         return (c % 2) * 16 + (c // 2 % 2) * 8 + (c // 4) * 4
 
-    def grams(c, carry):
-        gram, along = carry
+    def add_along(index):
+        index = index % 16
+        c, upper = index % 8, index // 8
+        total = along[upper]
+        for r in range(4):
+            total = total + bmm_nt(leaf[first_row(c) + r], slab3[c, r, pl.ds(upper * 128, 128), :])
+        along[upper] = total
+
+    def add_gram(c):
+        total = wide[...]
         for r in range(4):
             slab = slab3[c, r]
-            gram = gram + bmm_nt(slab, slab)
-            along = along + bmm_nt(leaf[first_row(c) + r], slab)
-        return gram, along
-
-    gram, along = lax.fori_loop(
-        0, 8, grams, (jnp.zeros((256, 256), F32), jnp.zeros((64, 256), F32))
-    )
+            total = total + bmm_nt(slab, slab)
+        wide[...] = total
+
+    ring = Ring(me, slab3, ring_sems, to)
+    along[...] = jnp.zeros_like(along)
+    wide[...] = jnp.zeros_like(wide)
+    ring.advance(1)
+    add_along(me)
+    for step in range(2, 10):
+        ring.advance(step)
+        distance = step - 1
+        add_along(me + distance)
+        if distance < 8:
+            add_along(me + 16 - distance)
+        if distance >= 4:
+            add_gram((me + distance) % 8)
+            if 4 < distance < 8:
+                add_gram((me + 16 - distance) % 8)
+    gram = wide[...]
     gram = jnp.concatenate([gram[:64] + gram[64:128], gram[128:192] + gram[192:]], axis=0)
     kernel = jnp.concatenate(
         [gram[:, :64] + gram[:, 64:128], gram[:, 128:192] + gram[:, 192:]], axis=1
-    )
-    along = jnp.concatenate(
-        [along[:, :64] + along[:, 64:128], along[:, 128:192] + along[:, 192:]], axis=1
     )
     basis, d_final = basis_of(kernel, start[...])
 
@@ -375,47 +450,48 @@
     damping = 0.1 * jnp.sum(d_final * eye, keepdims=True) / 64 + 1e-06
     capacitance = d_final + damping * eye
     inverse = eliminate(capacitance, jnp.concatenate([eye, jnp.zeros((64, 64), F32)], axis=1))[:, :64]
-    projected = mm_nt(along, basis)
+    sides = [along[i][:, :64] + along[i][:, 64:] for i in range(2)]
+    projected = mm_nt(jnp.concatenate(sides, axis=1), basis)
     weights = mm(mm_nt(projected, inverse), inverse)
     operand = split_basis(mm(weights, basis))
 
     def finish(c, carry):
         first = first_row(c)
         for r in range(0, 4, 2):
-            one = leaf[first + r].astype(F32) - merged(operand, slab3[c, r])
-            two = leaf[first + r + 1].astype(F32) - merged(operand, slab3[c, r + 1])
+            one, two = [
+                leaf[first + i].astype(F32)
+                - merged(operand, slab3[c, i])
+                for i in (r, r + 1)
+            ]
             where = (first + r) // 2
             out[:, pl.ds(pl.multiple_of(where * 128, 128), 128)] = jnp.concatenate([one[:, :64], two[:, :64]], axis=1)
             out[:, pl.ds(pl.multiple_of((where + 16) * 128, 128), 128)] = jnp.concatenate([one[:, 64:], two[:, 64:]], axis=1)
         return carry
 
     lax.fori_loop(0, 8, finish, 0)
+    ring.drain()
 
 
 def per_device(tokens, lengths, module_order):
-    by_module = jnp.transpose(tokens, (2, 0, 1, 3))
-    features = pl.pallas_call(
-        feature_kernel,
-        out_shape=jax.ShapeDtypeStruct((32, 2, 32, 128), BF16),
-        in_specs=[pl.BlockSpec(memory_space=SMEM)] * 2 + [pl.BlockSpec(memory_space=VMEM)],
-        out_specs=pl.BlockSpec(memory_space=VMEM),
-        name="features",
-    )(lengths, module_order, by_module)
-    rows = lax.all_to_all(features, "mod", split_axis=0, concat_axis=0, tiled=True)
-    leaf = jnp.transpose(rows.reshape(64, 32, 128), (1, 0, 2))
     dma = pltpu.SemaphoreType.DMA
     result = pl.pallas_call(
         tree_kernel,
         out_shape=jax.ShapeDtypeStruct((64, 4096), F32),
-        in_specs=[pl.BlockSpec(memory_space=VMEM)] * 2,
+        in_specs=[pl.BlockSpec(memory_space=SMEM)] * 2 + [pl.BlockSpec(memory_space=VMEM)] * 2,
         out_specs=pl.BlockSpec(memory_space=VMEM),
         scratch_shapes=[
+            pltpu.VMEM((32, 128, 128), BF16),
+            pltpu.VMEM((32, 2, 32, 128), BF16),
+            pltpu.VMEM((64, 32, 128), BF16),
+            pltpu.VMEM((32, 64, 128), BF16),
             pltpu.VMEM((16, 128, 128), BF16),
             pltpu.VMEM((8, 128, 128), BF16),
             pltpu.VMEM((8, 256, 128), BF16),
             pltpu.VMEM((4, 256, 128), BF16),
             pltpu.VMEM((8, 4, 256, 128), BF16),
-            pltpu.VMEM((4, 128, 128), BF16),
+            pltpu.VMEM((4, 64, 128), BF16),
+            pltpu.VMEM((4, 64, 128), BF16),
+            pltpu.VMEM((2, 64, 128), F32),
             pltpu.VMEM((32, 128), F32),
             pltpu.VMEM((32, 128), F32),
             pltpu.VMEM((96, 128), F32),
@@ -425,13 +501,14 @@
             pltpu.VMEM((2, 32, 128), F32),
             pltpu.VMEM((4, 32, 128), F32),
             pltpu.VMEM((8, 32, 128), F32),
-            dma((4,)), dma((4,)), dma((3,)), dma((3,)),
+            pltpu.VMEM((256, 256), F32),
+            dma((2, 32)), dma((2, 32)),
+            dma((5,)), dma((5,)), dma((3,)), dma((3,)),
             dma((2,)), dma((2,)), dma((4,)), dma((4,)), dma((8,)), dma((8,)),
-            dma((16,)), dma((16,)), dma((16,)), dma((16,)),
-        ],
+        ] + [dma((32,))] * 4,
         compiler_params=pltpu.CompilerParams(collective_id=0, has_side_effects=True),
         name="tree",
-    )(leaf, jnp.asarray(start_rows(128, 64)))
+    )(lengths, module_order, tokens, jnp.asarray(start_rows(128, 64)))
     return result[None]
 
 

time: 172 us -> 138 us (0.80)
  the two profiles are of different devices: /device:TPU:32 before, /device:TPU:2 now
where the time goes in v2:
time: 138 us
  Pallas kernels  135 us (98%)
  local copies, waits for them, and re-layouts  2.27 us (2%)
    pallas_call x1, Pallas kernels, per_device(): pl.pallas_call(tree_kernel, out_shape=jax.ShapeDtypeStruct((64, 4096), F3...  135 us

profile of v2, /device:TPU:2, one launch (start us, length us, event | category | flops | bytes accessed | tf_op | source)
XLA Modules:
  0.0 137.5 jit_solution(10423061979552838222)
XLA Ops:
  0.0 135.2 %tree.1 = f32[64,4096]{1,0:T(8,128)} custom-call(s32[2]{0:T(128)} %lengths.1, s32[32]{0:T(128)} %order.1, bf16[2,64,32,128]{3,2,1,0:T(8,128)(2,1)} %tokens.1, f32[64,128]{1,0:T(8,128)} %constant.2.clone.start), custom_call_target="tpu_custom_call" | custom-call | tf_op jit(solution)/shard_map/tree/pallas_call | solution.py:477
  135.2 2.3 %copy.6 = f32[1,64,4096]{2,1,0:T(8,128)} copy(f32[1,64,4096]{2,1,0:T(8,128)} %bitcast.1) | data formatting | bytes 2097152

commit v3 on v2

--- a/solution.py
+++ b/solution.py
@@ -143,35 +143,40 @@
         self.me, self.slabs, self.to = me, slabs, to
         self.sems = {True: sems[:2], False: sems[2:]}
 
-    def copy(self, step, part, rightward, arriving):
-        behind = step if arriving else step - 1
+    def copy(self, distance, part, rightward, arriving):
+        leg = 2 - distance % 2
+        behind = distance if arriving else distance - leg
         origin = (self.me + 16 - behind if rightward else self.me + behind) % 16
-        ref = self.slabs.at[origin % 8, part, pl.ds(origin // 8 * 128, 128), :]
+        ref = self.slabs.at[origin % 8, part, pl.ds(origin // 8 * 64, 64), :]
         send, recv = self.sems[rightward]
-        slot = (step - 1) * 4 + part
+        slot = (distance - 1) * 4 + part
         return pltpu.make_async_remote_copy(
             src_ref=ref, dst_ref=ref, send_sem=send.at[slot], recv_sem=recv.at[slot],
-            **self.to((self.me + (1 if rightward else 15)) % 16)
+            **self.to((self.me + (leg if rightward else 16 - leg)) % 16)
         )
 
     @staticmethod
-    def travels(step, part, rightward):
-        return step < 8 or (part < 2) == rightward
-
-    def advance(self, step):
-        for part in range(4):
-            for rightward in (True, False):
-                if step > 1 and self.travels(step - 1, part, rightward):
-                    self.copy(step - 1, part, rightward, True).wait_recv()
-                if step < 9 and self.travels(step, part, rightward):
-                    self.copy(step, part, rightward, False).start()
+    def travels(distance, part, rightward):
+        return distance < 8 or (part < 2) == rightward
+
+    def advance(self, stage, part):
+        for rightward in (True, False):
+            if stage > 1 and self.travels(2 * stage - 2, part, rightward):
+                self.copy(2 * stage - 2, part, rightward, True).wait_recv()
+            for distance in (2 * stage, 2 * stage - 1):
+                if stage < 5 and self.travels(distance, part, rightward):
+                    self.copy(distance, part, rightward, False).start()
+
+    def odd(self, stage, part):
+        for rightward in (True, False):
+            self.copy(2 * stage - 1, part, rightward, True).wait_recv()
 
     def drain(self):
-        for step in range(1, 9):
+        for distance in range(1, 9):
             for part in range(4):
                 for rightward in (True, False):
-                    if self.travels(step, part, rightward):
-                        self.copy(step, part, rightward, False).wait_send()
+                    if self.travels(distance, part, rightward):
+                        self.copy(distance, part, rightward, False).wait_send()
 
 
 def tree_kernel(
@@ -213,8 +218,8 @@
     lax.fori_loop(1, 32, greet, 0)
     for d in range(1, 8):
         pl.semaphore_signal(barrier, inc=1, **to(me // 8 * 8 + (me + d) % 8))
-    pl.semaphore_signal(barrier, inc=1, **to((me + 1) % 16))
-    pl.semaphore_signal(barrier, inc=1, **to((me + 15) % 16))
+    for d in (1, 2, 14, 15):
+        pl.semaphore_signal(barrier, inc=1, **to((me + d) % 16))
 
     for example in range(2):
         by_module[:, pl.ds(example * 64, 64), :] = jnp.transpose(tokens[example], (1, 0, 2))
@@ -230,7 +235,7 @@
         return carry
 
     lax.fori_loop(0, 2, make, 0)
-    pl.semaphore_wait(barrier, 40)
+    pl.semaphore_wait(barrier, 42)
 
     def delivery(d, half):
         target = (owner + d) % 32
@@ -399,49 +404,47 @@
 
     operand = split_basis(basis)
     column, side = me % 8, me // 8
+    ring = Ring(me, slab3, ring_sems, to)
     for r in range(4):
-        hi, lo = split2(merged(operand, slab2[r]))
-        slab3[column, r, pl.ds(side * 128, 64), :] = hi
-        slab3[column, r, pl.ds(side * 128 + 64, 64), :] = lo
+        slab3[column, r, pl.ds(side * 64, 64), :] = merged(operand, slab2[r]).astype(BF16)
+        ring.advance(1, r)
 
     def first_row(c):
         return (c % 2) * 16 + (c // 2 % 2) * 8 + (c // 4) * 4
 
-    def add_along(index):
+    def add_along(index, r):
         index = index % 16
         c, upper = index % 8, index // 8
-        total = along[upper]
-        for r in range(4):
-            total = total + bmm_nt(leaf[first_row(c) + r], slab3[c, r, pl.ds(upper * 128, 128), :])
-        along[upper] = total
-
-    def add_gram(c):
-        total = wide[...]
-        for r in range(4):
-            slab = slab3[c, r]
-            total = total + bmm_nt(slab, slab)
-        wide[...] = total
-
-    ring = Ring(me, slab3, ring_sems, to)
+        along[upper] += bmm_nt(leaf[first_row(c) + r], slab3[c, r, pl.ds(upper * 64, 64), :])
+
+    def add_gram(c, r):
+        slab = slab3[c, r]
+        wide[...] += bmm_nt(slab, slab)
+
+    def take(distance, r):
+        add_along(me + distance, r)
+        if 0 < distance < 8:
+            add_along(me + 16 - distance, r)
+        if distance >= 4:
+            add_gram((me + distance) % 8, r)
+            if 4 < distance < 8:
+                add_gram((me + 16 - distance) % 8, r)
+
     along[...] = jnp.zeros_like(along)
     wide[...] = jnp.zeros_like(wide)
-    ring.advance(1)
-    add_along(me)
-    for step in range(2, 10):
-        ring.advance(step)
-        distance = step - 1
-        add_along(me + distance)
-        if distance < 8:
-            add_along(me + 16 - distance)
-        if distance >= 4:
-            add_gram((me + distance) % 8)
-            if 4 < distance < 8:
-                add_gram((me + 16 - distance) % 8)
-    gram = wide[...]
-    gram = jnp.concatenate([gram[:64] + gram[64:128], gram[128:192] + gram[192:]], axis=0)
-    kernel = jnp.concatenate(
-        [gram[:, :64] + gram[:, 64:128], gram[:, 128:192] + gram[:, 192:]], axis=1
-    )
+    for stage in range(2, 6):
+        for r in range(4):
+            ring.advance(stage, r)
+            ring.odd(stage - 1, r)
+            if stage == 2:
+                take(0, r)
+            else:
+                take(2 * stage - 5, r)
+                take(2 * stage - 4, r)
+    for r in range(4):
+        take(7, r)
+        take(8, r)
+    kernel = wide[...]
     basis, d_final = basis_of(kernel, start[...])
 
     row = lax.broadcasted_iota(jnp.int32, (64, 64), 0)
@@ -450,10 +453,9 @@
     damping = 0.1 * jnp.sum(d_final * eye, keepdims=True) / 64 + 1e-06
     capacitance = d_final + damping * eye
     inverse = eliminate(capacitance, jnp.concatenate([eye, jnp.zeros((64, 64), F32)], axis=1))[:, :64]
-    sides = [along[i][:, :64] + along[i][:, 64:] for i in range(2)]
-    projected = mm_nt(jnp.concatenate(sides, axis=1), basis)
+    projected = mm_nt(jnp.concatenate([along[0], along[1]], axis=1), basis)
     weights = mm(mm_nt(projected, inverse), inverse)
-    operand = split_basis(mm(weights, basis))
+    operand = jnp.concatenate(split2(mm(weights, basis)), axis=0)
 
     def finish(c, carry):
         first = first_row(c)
@@ -468,7 +470,7 @@
             out[:, pl.ds(pl.multiple_of((where + 16) * 128, 128), 128)] = jnp.concatenate([one[:, 64:], two[:, 64:]], axis=1)
         return carry
 
-    lax.fori_loop(0, 8, finish, 0)
+    lax.fori_loop(0, 8, finish, 0, unroll=4)
     ring.drain()
 
 
@@ -488,10 +490,10 @@
             pltpu.VMEM((8, 128, 128), BF16),
             pltpu.VMEM((8, 256, 128), BF16),
             pltpu.VMEM((4, 256, 128), BF16),
-            pltpu.VMEM((8, 4, 256, 128), BF16),
+            pltpu.VMEM((8, 4, 128, 128), BF16),
             pltpu.VMEM((4, 64, 128), BF16),
             pltpu.VMEM((4, 64, 128), BF16),
-            pltpu.VMEM((2, 64, 128), F32),
+            pltpu.VMEM((2, 64, 64), F32),
             pltpu.VMEM((32, 128), F32),
             pltpu.VMEM((32, 128), F32),
             pltpu.VMEM((96, 128), F32),
@@ -501,7 +503,7 @@
             pltpu.VMEM((2, 32, 128), F32),
             pltpu.VMEM((4, 32, 128), F32),
             pltpu.VMEM((8, 32, 128), F32),
-            pltpu.VMEM((256, 256), F32),
+            pltpu.VMEM((128, 128), F32),
             dma((2, 32)), dma((2, 32)),
             dma((5,)), dma((5,)), dma((3,)), dma((3,)),
             dma((2,)), dma((2,)), dma((4,)), dma((4,)), dma((8,)), dma((8,)),

time: 138 us -> 126 us (0.913)
  Pallas kernels: 135 us -> 124 us
    pallas_call x1, Pallas kernels: 135 us -> 124 us  [per_device(): pl.pallas_call(tree_kernel, out_shape=jax.ShapeDtypeStruct((64, 4096), F3...]
where the time goes in v3:
time: 126 us
  Pallas kernels  124 us (98%)
  local copies, waits for them, and re-layouts  2.27 us (2%)
    pallas_call x1, Pallas kernels, per_device(): pl.pallas_call(tree_kernel, out_shape=jax.ShapeDtypeStruct((64, 4096), F3...  124 us

profile of v3, /device:TPU:2, one launch (start us, length us, event | category | flops | bytes accessed | tf_op | source)
XLA Modules:
  0.0 126.0 jit_solution(6673757516122400299)
XLA Ops:
  0.0 123.7 %tree.1 = f32[64,4096]{1,0:T(8,128)} custom-call(s32[2]{0:T(128)} %lengths.1, s32[32]{0:T(128)} %order.1, bf16[2,64,32,128]{3,2,1,0:T(8,128)(2,1)} %tokens.1, f32[64,128]{1,0:T(8,128)} %constant.2.clone.start), custom_call_target="tpu_custom_call" | custom-call | tf_op jit(solution)/shard_map/tree/pallas_call | solution.py:479
  123.7 2.3 %copy.6 = f32[1,64,4096]{2,1,0:T(8,128)} copy(f32[1,64,4096]{2,1,0:T(8,128)} %bitcast.1) | data formatting | bytes 2097152

commit v4 on v3

--- a/solution.py
+++ b/solution.py
@@ -66,32 +66,34 @@
 
     done = []
     for k in range(blocks):
-        p_left, p_right = left[k], right[k]
-        cols = [along_lanes(p_left, 8 * k + c) for c in range(8)]
+        cols = [along_lanes(left[k], 8 * k + c) for c in range(8)]
         below = {i: [along_lanes(left[i], 8 * k + c) for c in range(8)] for i in range(k + 1, blocks)}
+        corner = {(r, c): along_rows(cols[c], r) for c in range(8) for r in range(c, 8)}
+        row_left = [along_rows(left[k], r) for r in range(8)]
+        row_right = [along_rows(right[k], r) for r in range(8)]
         pivots = jnp.ones((8, 128), F32)
         reduced = jnp.zeros((8, 128), F32)
         for j in range(8):
-            col = cols[j]
-            pivot = along_rows(col, j)
-            inverse = 1.0 / pivot
-            here = sub == j
-            pivots = jnp.where(here, pivot, pivots)
-            row_right = along_rows(p_right, j)
-            reduced = jnp.where(here, row_right, reduced)
-            for c in range(j + 1, 8):
-                scaled = along_rows(cols[c], j) * inverse
-                cols[c] = jnp.where(here, scaled, cols[c] - col * scaled)
-            scaled = along_rows(p_left, j) * inverse
-            p_left = jnp.where(here, scaled, p_left - col * scaled)
-            scaled = row_right * inverse
-            p_right = jnp.where(here, scaled, p_right - col * scaled)
+            inverse = 1.0 / corner[j, j]
+            reduced = jnp.where(sub == j, row_right[j], reduced)
+            pivots = jnp.where(sub == j, corner[j, j], pivots)
+            factor = {r: corner[r, j] * inverse for r in range(j + 1, 8)}
+            scaled_left, scaled_right = row_left[j] * inverse, row_right[j] * inverse
+            for r in range(j + 1, 8):
+                for c in range(j + 1, r + 1):
+                    if c == r:
+                        corner[r, c] = corner[r, c] - (corner[r, j] * corner[c, j]) * inverse
+                    else:
+                        corner[r, c] = corner[r, c] - factor[r] * corner[c, j]
+                row_left[r] = row_left[r] - corner[r, j] * scaled_left
+                row_right[r] = row_right[r] - corner[r, j] * scaled_right
+            for i in range(k + 1, blocks):
+                col = below[i][j]
+                left[i] = left[i] - col * scaled_left
+                right[i] = right[i] - col * scaled_right
+                for c in range(j + 1, 8):
+                    below[i][c] = below[i][c] - col * factor[c]
         done.append(reduced * lax.rsqrt(pivots))
-        for c in range(8):
-            row_left, row_right = along_rows(p_left, c), along_rows(p_right, c)
-            for i in range(k + 1, blocks):
-                left[i] = left[i] - below[i][c] * row_left
-                right[i] = right[i] - below[i][c] * row_right
     return jnp.concatenate(done, axis=0)
 
 
@@ -100,8 +102,11 @@
         image = mm(basis, kernel)
         return eliminate(mm_nt(image, image), image)
 
-    basis = lax.fori_loop(0, ITERS, step, start)
-    return basis, mm_nt(mm(basis, kernel), basis)
+    return lax.fori_loop(0, ITERS, step, start)
+
+
+def gram_of(basis, kernel):
+    return mm_nt(mm(basis, kernel), basis)
 
 
 def pack(x):
@@ -181,7 +186,7 @@
 
 def tree_kernel(
     lengths, order, tokens, start, out,
-    by_module, features, rows, leaf,
+    by_module, features, rows, rows_over, leaf,
     pair, quad, slab1, slab2, slab3, send2h, send2l, along,
     d0_out, d0_in, qd_out, qd_in, d2_out, d2_in,
     x0, x1, x2, wide,
@@ -209,10 +214,16 @@
         copy.start()
         return copy
 
+    def over(index):
+        return dict(device_id={"grp": sister0, "mod": index}, device_id_type=pl.DeviceIdType.MESH)
+
     barrier = pltpu.get_barrier_semaphore()
+    pl.semaphore_signal(barrier, inc=1, **over(owner))
 
     def greet(d, carry):
-        pl.semaphore_signal(barrier, inc=1, **across((owner + d) % 32))
+        target = (owner + d) % 32
+        pl.semaphore_signal(barrier, inc=1, **across(target))
+        pl.semaphore_signal(barrier, inc=1, **over(target))
         return carry
 
     lax.fori_loop(1, 32, greet, 0)
@@ -235,54 +246,51 @@
         return carry
 
     lax.fori_loop(0, 2, make, 0)
-    pl.semaphore_wait(barrier, 42)
-
-    def delivery(d, half):
+    pl.semaphore_wait(barrier, 74)
+
+    def delivery(d):
         target = (owner + d) % 32
-        columns = pl.ds(half * 16, 16)
         return pltpu.make_async_remote_copy(
-            src_ref=features.at[target, :, columns], dst_ref=rows.at[pl.ds(owner * 2, 2), columns],
-            send_sem=to_owner.at[half, target], recv_sem=at_owner.at[half, owner], **across(target)
+            src_ref=features.at[target], dst_ref=rows.at[pl.ds(owner * 2, 2)],
+            send_sem=to_owner.at[0, target], recv_sem=at_owner.at[0, owner], **across(target)
         )
 
-    def arrival(d, half):
+    def arrival(d):
         source = (owner + d) % 32
-        columns = pl.ds(half * 16, 16)
         return pltpu.make_async_remote_copy(
-            src_ref=features.at[source, :, columns], dst_ref=rows.at[pl.ds(source * 2, 2), columns],
-            send_sem=to_owner.at[half, source], recv_sem=at_owner.at[half, source], **across(source)
+            src_ref=features.at[source], dst_ref=rows.at[pl.ds(source * 2, 2)],
+            send_sem=to_owner.at[0, source], recv_sem=at_owner.at[0, source], **across(source)
         )
 
-    for half in (1 - b0, b0):
-        def deliver(d, carry):
-            delivery(d, half).start()
-            return carry
-
-        lax.fori_loop(1, 32, deliver, 0)
+    def delivery_over(d):
+        target = (owner + d) % 32
+        return pltpu.make_async_remote_copy(
+            src_ref=features.at[target, :, pl.ds((1 - b0) * 16, 16)], dst_ref=rows_over.at[pl.ds(owner * 2, 2)],
+            send_sem=to_owner.at[1, target], recv_sem=at_owner.at[1, owner], **over(target)
+        )
+
+    def arrival_over(d):
+        source = (owner + d) % 32
+        return pltpu.make_async_remote_copy(
+            src_ref=features.at[source, :, pl.ds((1 - b0) * 16, 16)], dst_ref=rows_over.at[pl.ds(source * 2, 2)],
+            send_sem=to_owner.at[1, source], recv_sem=at_owner.at[1, source], **over(source)
+        )
+
+    def deliver(d, carry):
+        delivery_over(d).start()
+        delivery(d).start()
+        return carry
+
+    lax.fori_loop(1, 32, deliver, 0)
+    delivery_over(0).start()
     rows[pl.ds(owner * 2, 2)] = features[owner]
 
-    def collect(half):
-        def one(d, carry):
-            arrival(d, half).wait_recv()
-            return carry
-
-        lax.fori_loop(1, 32, one, 0)
-        leaf[pl.ds(half * 16, 16)] = jnp.transpose(rows[:, pl.ds(half * 16, 16)], (1, 0, 2))
-
-    collect(1 - b0)
-
-    leaf_copy = send(
-        leaf.at[pl.ds((1 - b0) * 16, 16)], pair.at[:, pl.ds(b0 * 64, 64), :],
-        bulk_send, bulk_recv, 0, 0, sister0,
-    )
-    collect(b0)
-
-    def sent(d, carry):
-        delivery(d, 0).wait_send()
-        delivery(d, 1).wait_send()
-        return carry
-
-    lax.fori_loop(1, 32, sent, 0)
+    def collect(d, carry):
+        arrival(d).wait_recv()
+        return carry
+
+    lax.fori_loop(1, 32, collect, 0)
+    leaf[...] = jnp.transpose(rows[...], (1, 0, 2))
 
     def own_gram(r, acc):
         slab = leaf[r]
@@ -291,19 +299,22 @@
     d_own = lax.fori_loop(0, 32, own_gram, jnp.zeros((64, 64), F32), unroll=8)
     d0_out[...] = pack(d_own)
     d_copy = send(d0_out, d0_in, small_send, small_recv, 0, 0, sister0)
-    pair[:, pl.ds(b0 * 64, 64), :] = leaf[pl.ds(b0 * 16, 16)]
-
     early = []
     for other in range(2):
         target = sister1 - b0 + other
         offset = other * 16 + (1 - b1) * 8
-        early.append((
+        early.append(send(
             leaf.at[pl.ds(offset, 8)], quad.at[:, pl.ds(b0 * 64, 64), :],
             bulk_send, bulk_recv, 1 + other, 1 + b0, target,
         ))
-    leaf_copy.wait()
-    early = [send(*args) for args in early]
-    d_copy.wait()
+    pair[:, pl.ds(b0 * 64, 64), :] = leaf[pl.ds(b0 * 16, 16)]
+
+    def collect_over(d, carry):
+        arrival_over(d).wait_recv()
+        return carry
+
+    lax.fori_loop(0, 32, collect_over, 0)
+    pair[:, pl.ds((1 - b0) * 64, 64), :] = jnp.transpose(rows_over[...], (1, 0, 2))
 
     def reduce_cross(partial, box, sems, recvs, members):
         mine = me % members
@@ -332,12 +343,23 @@
 
     cross = lax.fori_loop(0, 16, cross0, jnp.zeros((64, 64), F32), unroll=8)
     cross = reduce_cross(cross, x0, x0_send, x0_recv, 2)
+    d_copy.wait()
+
+    def sent(d, carry):
+        delivery(d).wait_send()
+        delivery_over(d).wait_send()
+        return carry
+
+    lax.fori_loop(1, 32, sent, 0)
+    delivery_over(0).wait_send()
     d_sister = unpack(d0_in[...])
     kernel = assemble(jnp.where(b0 == 0, d_own, d_sister), cross, jnp.where(b0 == 0, d_sister, d_own))
-    basis, d_own = basis_of(kernel, start[...])
+    basis = basis_of(kernel, start[...])
     qd_out[:64] = basis
+    q_copy = send(qd_out.at[:64], qd_in.at[:64], small_send, small_recv, 1, 1, sister1)
+    d_own = gram_of(basis, kernel)
     qd_out[64:] = pack(d_own)
-    qd_copy = send(qd_out, qd_in, small_send, small_recv, 1, 1, sister1)
+    d_copy = send(qd_out.at[64:], qd_in.at[64:], small_send, small_recv, 3, 3, sister1)
 
     def merged0(b, slabs, first, side):
         operand = jnp.concatenate(split3(b), axis=0)
@@ -360,8 +382,9 @@
             src_ref=leaf.at[pl.ds(0, 8)], dst_ref=quad.at[:, pl.ds(other * 64, 64), :],
             send_sem=bulk_send.at[1 + other], recv_sem=bulk_recv.at[1 + other], **to(sister1 - b0 + other)
         ).wait_recv()
-    qd_copy.wait()
+    q_copy.wait()
     merged0(qd_in[:64], quad, 0, 1 - b1)
+    d_copy.wait()
     d_sister = unpack(qd_in[64:])
 
     def cross1(r, acc):
@@ -372,8 +395,7 @@
     cross = acc[:64, :64] + acc[:64, 64:] + acc[64:, :64] + acc[64:, 64:]
     cross = reduce_cross(cross, x1, x1_send, x1_recv, 4)
     kernel = assemble(jnp.where(b1 == 0, d_own, d_sister), cross, jnp.where(b1 == 0, d_sister, d_own))
-    basis, d_own = basis_of(kernel, start[...])
-    d2_out[...] = pack(d_own)
+    basis = basis_of(kernel, start[...])
 
     def merged(operand, slab):
         product = bmm(operand, slab)
@@ -385,6 +407,8 @@
         send2h[r] = hi
         send2l[r] = lo
     hi_copy = send(send2h, slab2.at[:, pl.ds(b2 * 128, 64), :], bulk_send, bulk_recv, 3, 3, sister2)
+    d_own = gram_of(basis, kernel)
+    d2_out[...] = pack(d_own)
     d_copy = send(d2_out, d2_in, small_send, small_recv, 2, 2, sister2)
     for r in range(4):
         hi, lo = split2(merged(operand, slab1[b2 * 4 + r]))
@@ -399,7 +423,7 @@
     cross = reduce_cross(cross, x2, x2_send, x2_recv, 8)
     lo_copy = send(send2l, slab2.at[:, pl.ds(b2 * 128 + 64, 64), :], bulk_send, bulk_recv, 4, 4, sister2)
     kernel = assemble(jnp.where(b2 == 0, d_own, d_sister), cross, jnp.where(b2 == 0, d_sister, d_own))
-    basis, _ = basis_of(kernel, start[...])
+    basis = basis_of(kernel, start[...])
     lo_copy.wait()
 
     operand = split_basis(basis)
@@ -445,7 +469,8 @@
         take(7, r)
         take(8, r)
     kernel = wide[...]
-    basis, d_final = basis_of(kernel, start[...])
+    basis = basis_of(kernel, start[...])
+    d_final = gram_of(basis, kernel)
 
     row = lax.broadcasted_iota(jnp.int32, (64, 64), 0)
     col = lax.broadcasted_iota(jnp.int32, (64, 64), 1)
@@ -485,6 +510,7 @@
             pltpu.VMEM((32, 128, 128), BF16),
             pltpu.VMEM((32, 2, 32, 128), BF16),
             pltpu.VMEM((64, 32, 128), BF16),
+            pltpu.VMEM((64, 16, 128), BF16),
             pltpu.VMEM((32, 64, 128), BF16),
             pltpu.VMEM((16, 128, 128), BF16),
             pltpu.VMEM((8, 128, 128), BF16),
@@ -505,7 +531,7 @@
             pltpu.VMEM((8, 32, 128), F32),
             pltpu.VMEM((128, 128), F32),
             dma((2, 32)), dma((2, 32)),
-            dma((5,)), dma((5,)), dma((3,)), dma((3,)),
+            dma((5,)), dma((5,)), dma((4,)), dma((4,)),
             dma((2,)), dma((2,)), dma((4,)), dma((4,)), dma((8,)), dma((8,)),
         ] + [dma((32,))] * 4,
         compiler_params=pltpu.CompilerParams(collective_id=0, has_side_effects=True),

time: 126 us -> 122 us (0.968)
  the two profiles are of different devices: /device:TPU:2 before, /device:TPU:24 now
where the time goes in v4:
time: 122 us
  Pallas kernels  119 us (98%)
  local copies, waits for them, and re-layouts  2.27 us (2%)
    pallas_call x1, Pallas kernels, per_device(): pl.pallas_call(tree_kernel, out_shape=jax.ShapeDtypeStruct((64, 4096), F3...  119 us

profile of v4, /device:TPU:24, one launch (start us, length us, event | category | flops | bytes accessed | tf_op | source)
XLA Modules:
  0.0 121.7 jit_solution(6860228669432210016)
XLA Ops:
  0.0 119.5 %tree.1 = f32[64,4096]{1,0:T(8,128)} custom-call(s32[2]{0:T(128)} %lengths.1, s32[32]{0:T(128)} %order.1, bf16[2,64,32,128]{3,2,1,0:T(8,128)(2,1)} %tokens.1, f32[64,128]{1,0:T(8,128)} %constant.2.clone.start), custom_call_target="tpu_custom_call" | custom-call | tf_op jit(solution)/shard_map/tree/pallas_call | solution.py:504
  119.5 2.3 %copy.6 = f32[1,64,4096]{2,1,0:T(8,128)} copy(f32[1,64,4096]{2,1,0:T(8,128)} %bitcast.1) | data formatting | bytes 2097152
